TPU v7x, 256 devices: a whole 4x4x8 slice. The times are simulated.
256 devices in a mesh: ctx: 16 (over z, core), exp: 16 (over x, y).
Axes of the slice: x: 4, y: 4, z: 8, core: 2. Of those that a mesh axis runs over, the one named last changes fastest.
Arguments:
- queries: bfloat16 [2, 16384, 2560], P(None, ('ctx', 'exp'))
- key_states: bfloat16 [2, 16384, 512], P(None, ('ctx', 'exp'))
- value_state_rows: bfloat16 [2, 16384, 512], P(None, ('ctx', 'exp')), may hold values from -6 to 6
- block_lists: int32 [32], replicated, may hold values from 0 to 31, as said below
- hidden: bfloat16 [8192, 5120], P(('ctx', 'exp')), may hold values from -8 to 8
- router: bfloat16 [5120, 16], replicated, may hold values from -0.078125 to 0.078125
- expert_ids: int32 [8192, 1], P(('ctx', 'exp')), may hold values from 0 to 15; in each aligned block of 32 rows (0 to 31, 32 to 63, ...) at most 4 rows name the same one
- w_gate: bfloat16 [16, 5120, 4096], P('exp', None, 'ctx'), may hold values from -0.078125 to 0.078125
- w_up: bfloat16 [16, 5120, 4096], P('exp', None, 'ctx'), may hold values from -0.078125 to 0.078125
- w_down: bfloat16 [16, 4096, 5120], P('exp', 'ctx'), may hold values from -0.1875 to 0.1875
Outputs:
- attention: bfloat16 [2, 16384, 2560], P(None, ('ctx', 'exp'))
- moe_out: bfloat16 [8192, 5120], P(('ctx', 'exp'))
Inputs may be any that keep to these rules, and one draw needn't show every extreme that they name: block_lists[b] is a block before b, or b itself when block b attends only to its own keys (always for b = 0 and for b = 31). Block p is held by index min(p, 31 - p) of ctx; for each d < 16 with block_lists[d] != d and block_lists[31 - d] != 31 - d, the two listed blocks are held by different indices. `expert_ids`: among the rows of one device no expert is named more than 4 times.
All inputs are finite; a program needn't handle non-finite values.
Results may differ from a plain program's by a relative error of at most 0.023.
Values may be sent and summed in bfloat16 or wider, within the bound.
No kernel may reach another device: no remote copies, remote signals or barrier semaphores. Data moves between devices by JAX's collectives and lax.ppermute only.
A program may use at most 128 MiB of HBM per device.

v0:
```python
import jax
import jax.numpy as jnp
from jax import lax
from jax.sharding import PartitionSpec as P

QUERY_HEADS = 20
KEY_HEADS = 4
HEAD_DIM = 128
NEGATIVE_LARGE = -1e30


def attend_all(queries, key_states, value_state_rows, block_lists):
    ctx_count = lax.axis_size("ctx")
    blocks_total = 2 * ctx_count
    ctx_index = lax.axis_index("ctx")
    exp_index = lax.axis_index("exp")
    row_total_count = queries.shape[1]
    query_group_width = QUERY_HEADS // KEY_HEADS
    key_value_width = KEY_HEADS * HEAD_DIM
    paired = jnp.concatenate([key_states, value_state_rows], axis=2)
    own_blocks = jnp.stack([ctx_index, blocks_total - 1 - ctx_index])
    listed = block_lists[own_blocks]
    usable = listed != own_blocks
    holder = jnp.minimum(listed, blocks_total - 1 - listed)
    everyone = lax.all_gather(paired[None], "ctx", axis=0, tiled=True)
    second_half = (listed >= ctx_count).astype(jnp.int32)
    remote = everyone[holder, second_half]
    stacked = jnp.concatenate([paired, remote], axis=0)
    query_head_rows = queries.reshape(2, row_total_count, KEY_HEADS, query_group_width, HEAD_DIM)
    query_pos = exp_index * row_total_count + jnp.arange(row_total_count)
    scaling = HEAD_DIM ** (-0.5)
    piece_rows = lax.all_gather(stacked, "exp", axis=1, tiled=True)
    running_maximum = jnp.full(
        (2, KEY_HEADS, query_group_width, row_total_count), NEGATIVE_LARGE, jnp.float32
    )
    key_total_count = piece_rows.shape[1]
    concatenated_rows = jnp.concatenate([piece_rows[0:2], piece_rows[2:4]], axis=1)
    key_portion = concatenated_rows[..., :key_value_width].reshape(
        2, 2 * key_total_count, KEY_HEADS, HEAD_DIM
    )
    value_portion = concatenated_rows[..., key_value_width:].reshape(
        2, 2 * key_total_count, KEY_HEADS, HEAD_DIM
    )
    scores = (
        jnp.einsum(
            "prhgd,pkhd->phgrk", query_head_rows, key_portion, preferred_element_type=jnp.float32
        )
        * scaling
    )
    key_pos = jnp.arange(key_total_count)
    causal = jnp.broadcast_to(
        (key_pos[None, :] <= query_pos[:, None])[None], (2, row_total_count, key_total_count)
    )
    listed_ok = jnp.broadcast_to(usable[:, None, None], (2, row_total_count, key_total_count))
    allowed = jnp.concatenate([causal, listed_ok], axis=2)[:, None, None]
    masked = jnp.where(allowed, scores, NEGATIVE_LARGE)
    new_max = jnp.maximum(running_maximum, jnp.max(masked, axis=-1))
    weights = jnp.where(allowed, jnp.exp(masked - new_max[..., None]), 0.0)
    new_sum = jnp.sum(weights, axis=-1)
    update = jnp.einsum(
        "phgrk,pkhd->phgrd",
        weights.astype(jnp.bfloat16),
        value_portion,
        preferred_element_type=jnp.float32,
    )
    mixed_rows = update / new_sum[..., None]
    return (
        jnp.transpose(mixed_rows, (0, 3, 1, 2, 4))
        .reshape(2, row_total_count, QUERY_HEADS * HEAD_DIM)
        .astype(jnp.bfloat16)
    )


def route_experts(hidden, router, expert_ids, w_gate, w_up, w_down):
    expert_table = router.shape[1]
    local_tokens = hidden.shape[0]
    model_width = hidden.shape[1]
    capacity = max(2, 2 * local_tokens // expert_table)
    exp_count = lax.axis_size("exp")
    logits = jnp.dot(hidden, router, preferred_element_type=jnp.float32)
    selected_expert = expert_ids[:, 0]
    onehot = (selected_expert[:, None] == jnp.arange(expert_table)[None, :]).astype(jnp.float32)
    gate_score = jax.nn.sigmoid(jnp.sum(logits * onehot, axis=1))
    scaled_scores = (hidden.astype(jnp.float32) * gate_score[:, None]).astype(jnp.bfloat16)
    slot_rank = (jnp.sum(jnp.cumsum(onehot, axis=0) * onehot, axis=1) - 1.0).astype(jnp.int32)
    dispatch = (
        (selected_expert[None, None, :] == jnp.arange(expert_table)[:, None, None])
        & (slot_rank[None, None, :] == jnp.arange(capacity)[None, :, None])
    ).astype(jnp.bfloat16)
    gate_local = w_gate[0]
    up_local = w_up[0]
    down_local = w_down[0]
    outgoing = jnp.einsum(
        "ect,td->ecd", dispatch, scaled_scores, preferred_element_type=jnp.float32
    ).astype(jnp.bfloat16)
    incoming = lax.all_to_all(outgoing, "exp", split_axis=0, concat_axis=0, tiled=True)
    piece_rows = lax.all_gather(incoming.reshape(-1, model_width), "ctx", axis=0, tiled=True)
    gate_part = jnp.dot(piece_rows, gate_local, preferred_element_type=jnp.float32)
    up_part = jnp.dot(piece_rows, up_local, preferred_element_type=jnp.float32)
    hidden_activation = (jax.nn.silu(gate_part) * up_part).astype(jnp.bfloat16)
    summed_output = lax.psum_scatter(
        jnp.dot(hidden_activation, down_local, preferred_element_type=jnp.float32).astype(
            jnp.bfloat16
        ),
        "ctx",
        scatter_dimension=0,
        tiled=True,
    )
    returned = lax.all_to_all(
        summed_output.reshape(exp_count, capacity, model_width),
        "exp",
        split_axis=0,
        concat_axis=0,
        tiled=True,
    )
    return jnp.einsum("ect,ecd->td", dispatch, returned, preferred_element_type=jnp.float32).astype(
        jnp.bfloat16
    )


def shards(
    queries,
    key_states,
    value_state_rows,
    block_lists,
    hidden,
    router,
    expert_ids,
    w_gate,
    w_up,
    w_down,
):
    attention = attend_all(queries, key_states, value_state_rows, block_lists)
    moe_out = route_experts(hidden, router, expert_ids, w_gate, w_up, w_down)
    return (attention, moe_out)


def solution(mesh):
    placed = (
        P(None, ("ctx", "exp"), None),
        P(None, ("ctx", "exp"), None),
        P(None, ("ctx", "exp"), None),
        P(),
        P(("ctx", "exp"), None),
        P(),
        P(("ctx", "exp"), None),
        P("exp", None, "ctx"),
        P("exp", None, "ctx"),
        P("exp", "ctx", None),
    )
    return jax.shard_map(
        shards,
        mesh=mesh,
        in_specs=placed,
        out_specs=(P(None, ("ctx", "exp"), None), P(("ctx", "exp"), None)),
        check_vma=False,
    )
```

profile of v0, /device:TPU:2, one launch (start us, length us, event | category | flops | bytes accessed | tf_op | source)
XLA Modules:
  0.0 308.0 jit_solution(14980662462300857561)
XLA Ops:
  7.2 0.0 all-gather.9.cloned.1.call-start
  7.2 1.1 constant_dynamic-update-slice_fusion.1
  8.3 0.9 constant_dynamic-update-slice_fusion
  9.2 0.7 copy-done.2
  9.9 0.0 all-gather.9.cloned.1.call-update
  9.9 0.0 all-gather.7.cloned.1.call-start
  10.0 0.7 fusion.45
  10.7 0.1 copy.28
  10.7 0.1 reduce_window_sum.11
  10.8 0.1 copy.29
  10.9 0.7 select_reduce_fusion
  11.5 1.3 fusion.24
  12.9 0.7 iota_compare_fusion.2
  13.5 1.4 convolution_convert_fusion.1
  14.9 0.5 copy.30
  15.4 18.6 %all_to_all.10 = bf16[16,4,5120]{2,1,0:T(4,128)(2,1)S(1)} all-to-all(bf16[16,4,5120]{2,1,0:T(4,128)(2,1)S(1)} %copy.30), channel_id=1, replica_groups=mesh['ctx'=16,'exp'=16] {'exp'}, dimensions={0} | all-to-all | bytes 1310720 | tf_op jit(solution)/shard_map/all_to_all | solution.py:96
  34.0 1.0 reshape.252
  35.0 0.0 all-gather.7.cloned.1.call-update
  35.0 0.0 all-gather.5.cloned.1.call-start
  35.1 0.1 fusion.46
  35.2 1.3 gather_fusion
  36.5 19.3 %all-gather.9.cloned.1.call-done = bf16[32,64,1024]{2,1,0:T(8,128)(2,1)} async-done(((bf16[2,64,1024]{2,1,0:T(8,128)(2,1)}), bf16[32,64,1024]{2,1,0:T(8,128)(2,1)}) %all-gather.9.cloned.1.call-update) | async-done | bytes 4194320 | tf_op jit(solution)/shard_map/all_gather | solution.py:25
  55.8 2.8 gather_fusion.1
  58.5 1.8 pad_maximum_fusion.1
  60.3 0.0 all-gather.5.cloned.1.call-update
  60.3 0.0 reduce-scatter.2.cloned.1.call-start
  60.4 61.9 %all-gather.7.cloned.1.call-done = bf16[1024,5120]{1,0:T(8,128)(2,1)} async-done(((bf16[64,5120]{1,0:T(8,128)(2,1)}), bf16[1024,5120]{1,0:T(8,128)(2,1)}) %all-gather.7.cloned.1.call-update) | async-done | bytes 10485776 | tf_op jit(solution)/shard_map/all_gather | solution.py:97
  122.3 8.6 %fusion.11 = f32[1024,256]{1,0:T(8,128)} fusion(bf16[1024,5120]{1,0:T(8,128)(2,1)} %all-gather.7.cloned.1.call-done, bf16[1,5120,256]{2,1,0:T(8,128)(2,1)} %param.17), kind=kOutput, calls=%fused_computation.20 | convolution fusion | flops 2684354560 | bytes 14155776 | tf_op jit(solution)/shard_map/dot_general | solution.py:98
  130.9 21.1 %convolution_convert_fusion = bf16[1024,5120]{1,0:T(8,128)(2,1)} fusion(bf16[1,256,5120]{2,1,0:T(8,128)(2,1)S(1)} %copy-done, bf16[1024,5120]{1,0:T(8,128)(2,1)} %all-gather.7.cloned.1.call-done, bf16[1,5120,256]{2,1,0:T(8,128)(2,1)} %param.18, f32[1024,256]{1,0:T(8,128)} %fusion.11), kind=kOutput, calls=%fused_computation.9 | convolution fusion | flops 5375524864 | bytes 27262976 | tf_op jit(solution)/shard_map/dot_general | solution.py:102
  152.0 1.1 copy-done.3
  153.1 0.8 reshape.250
  153.9 0.1 add_compare_fusion
  153.9 0.1 iota_compare_fusion
  154.1 0.1 broadcast_in_dim.27
  154.2 44.9 %all-gather.5.cloned.1.call-done = bf16[4,1024,1024]{2,1,0:T(8,128)(2,1)} async-done(((bf16[4,64,1024]{2,1,0:T(8,128)(2,1)}), bf16[4,1024,1024]{2,1,0:T(8,128)(2,1)}) %all-gather.5.cloned.1.call-update) | async-done | bytes 8388624 | tf_op jit(solution)/shard_map/all_gather | solution.py:32
  199.1 3.9 %fusion.57 = (bf16[2,1024,1024]{2,1,0:T(8,128)(2,1)S(1)}, bf16[2,1024,1024]{2,1,0:T(8,128)(2,1)S(1)}) fusion(bf16[4,1024,1024]{2,1,0:T(8,128)(2,1)} %all-gather.5.cloned.1.call-done), kind=kLoop, calls=%fused_computation.78 | loop fusion | bytes 16777216 | tf_op jit(solution)/shard_map/slice | solution.py:37
  203.1 3.7 %fusion.7 = (bf16[2,2048,512]{2,1,0:T(8,128)(2,1)}, bf16[2,2048,512]{2,1,0:T(8,128)(2,1)}) fusion(bf16[2,1024,1024]{2,1,0:T(8,128)(2,1)S(1)} %get-tuple-element.4, bf16[2,1024,1024]{2,1,0:T(8,128)(2,1)S(1)} %get-tuple-element.5), kind=kLoop, calls=%fused_computation.15 | loop fusion | flops 16777216 | bytes 16777216 | tf_op jit(solution)/shard_map/concatenate | solution.py:37
  206.8 6.3 %copy.25 = bf16[2,2048,512]{1,2,0:T(8,128)(2,1)} copy(bf16[2,2048,512]{2,1,0:T(8,128)(2,1)} %get-tuple-element.3) | data formatting | bytes 8388608 | tf_op jit(solution)/shard_map/slice | solution.py:41
  213.1 6.3 %copy.22 = bf16[2,2048,512]{1,2,0:T(8,128)(2,1)} copy(bf16[2,2048,512]{2,1,0:T(8,128)(2,1)} %get-tuple-element.2) | data formatting | bytes 8388608 | tf_op jit(solution)/shard_map/slice | solution.py:38
  219.4 13.4 %fusion = (f32[2,4,5,64]{3,2,1,0:T(8,128)S(1)}, f32[2,4,2048,64,5]{2,3,4,1,0:T(8,128)}) fusion(pred[2,64,2048]{2,1,0:T(8,128)(4,1)S(1)} %pad_add_fusion, bf16[2,2048,4,128,1]{1,3,4,2,0:T(8,128)(2,1)} %bitcast.70, bf16[2,64,4,5,128]{4,3,2,1,0:T(8,128)(2,1)S(1)} %reshape.250), kind=kOutput, calls=%fused_computation.4 | convolution fusion | flops 1357903360 | bytes 26093568 | tf_op jit(solution)/shard_map/prhgd,pkhd->phgrk/dot_general | solution.py:45
  232.9 11.6 %fusion.1 = f32[2,4,5,64]{3,2,1,0:T(8,128)} fusion(f32[2,4,2048,64,5]{2,3,4,1,0:T(8,128)} %get-tuple-element.7, f32[2,4,5,64]{3,2,1,0:T(8,128)S(1)} %broadcast_maximum_fusion, pred[2,64,2048]{2,1,0:T(8,128)(4,1)S(1)} %pad_add_fusion), kind=kLoop, calls=%fused_computation.5 | loop fusion | flops 26211840 | bytes 21254144 | tf_op jit(solution)/shard_map/reduce_sum | solution.py:59
  244.5 31.3 %reduce-scatter.2.cloned.1.call-done = bf16[64,5120]{1,0:T(8,128)(2,1)} async-done(((bf16[1024,5120]{1,0:T(8,128)(2,1)}), bf16[64,5120]{1,0:T(8,128)(2,1)}) %reduce-scatter.2.cloned.1.call-update) | async-done | bytes 655376 | tf_op jit(solution)/shard_map/reduce_scatter | solution.py:101
  275.8 2.4 reshape.253
  278.2 7.4 %all-to-all-start.1 = ((bf16[16,4,5120]{2,1,0:T(4,128)(2,1)}), bf16[16,4,5120]{2,1,0:T(4,128)(2,1)S(1)}, u32[]{:S(2)}, u32[]{:S(2)}) async-start(bf16[16,4,5120]{2,1,0:T(4,128)(2,1)} %reshape.253), calls=%async_computation.2 | async-start | bytes 1310720 | tf_op jit(solution)/shard_map/all_to_all | solution.py:109
  285.5 10.9 %divide_convert_fusion = bf16[2,64,4,5,128]{4,1,3,2,0:T(8,128)(2,1)S(1)} fusion(bf16[2,2048,4,128,1]{1,3,4,2,0:T(8,128)(2,1)} %bitcast.71, f32[2,4,2048,64,5]{2,3,4,1,0:T(8,128)} %get-tuple-element.7, f32[2,4,5,64]{3,2,1,0:T(8,128)} %copy-done.4, pred[2,64,2048]{2,1,0:T(8,128)(4,1)S(1)} %pad_add_fusion, f32[2,64,4,5]{1,3,2,0:T(8,128)} %bitcast.72), kind=kOutput, calls=%fused_computation.23 | convolution fusion | flops 1369047040 | bytes 26103808 | tf_op jit(solution)/shard_map/phgrk,pkhd->phgrd/dot_general | solution.py:60
  296.4 1.4 copy.27
  297.9 2.6 convert_element_type.51
  300.4 1.0 fusion.6
  (19 shorter events, 0.1 us)
Async XLA Ops:
  7.2 123.7 %copy-start = (bf16[1,256,5120]{2,1,0:T(8,128)(2,1)S(1)}, bf16[1,256,5120]{2,1,0:T(8,128)(2,1)}, u32[]{:S(2)}) copy-start(bf16[1,256,5120]{2,1,0:T(8,128)(2,1)} %param.19) | copy-start | bytes 7864324
  7.2 48.6 %all-gather.9.cloned.1.call-start = ((), (), s32[]{:S(2)}) async-start(), calls=%async_computation.6 | async-start | bytes 4456448 | tf_op jit(solution)/shard_map/all_gather | solution.py:25
  9.2 0.7 copy-start.2
  9.9 112.4 %all-gather.7.cloned.1.call-start = ((), (), s32[]{:S(2)}) async-start(), calls=%async_computation.4 | async-start | bytes 11141120 | tf_op jit(solution)/shard_map/all_gather | solution.py:97
  35.0 164.1 %all-gather.5.cloned.1.call-start = ((), (), s32[]{:S(2)}) async-start(), calls=%async_computation.3 | async-start | bytes 8912896 | tf_op jit(solution)/shard_map/all_gather | solution.py:32
  60.3 215.5 %reduce-scatter.2.cloned.1.call-start = ((), (), s32[]{:S(2)}) async-start(), calls=%async_computation.5 | async-start | bytes 11141120 | tf_op jit(solution)/shard_map/reduce_scatter | solution.py:101
  152.0 1.1 copy-start.3
  232.9 11.6 %copy-start.4 = (f32[2,4,5,64]{3,2,1,0:T(8,128)}, f32[2,4,5,64]{3,2,1,0:T(8,128)S(1)}, u32[]{:S(2)}) copy-start(f32[2,4,5,64]{3,2,1,0:T(8,128)S(1)} %broadcast_maximum_fusion) | copy-start | bytes 30724
  278.2 22.3 %all-to-all-start.1 = ((bf16[16,4,5120]{2,1,0:T(4,128)(2,1)}), bf16[16,4,5120]{2,1,0:T(4,128)(2,1)S(1)}, u32[]{:S(2)}, u32[]{:S(2)}) async-start(bf16[16,4,5120]{2,1,0:T(4,128)(2,1)} %reshape.253), calls=%async_computation.2 | async-start | bytes 1310720 | tf_op jit(solution)/shard_map/all_to_all | solution.py:109
  285.5 15.9 %copy-start.1 = (bf16[1,256,5120]{2,1,0:T(8,128)(2,1)S(1)}, bf16[1,256,5120]{2,1,0:T(8,128)(2,1)}, u32[]{:S(2)}) copy-start(bf16[1,256,5120]{2,1,0:T(8,128)(2,1)} %param.19) | copy-start | bytes 7864324
Sparse Core Ops, SparseCore 0:
  10.4 45.3 all-gather.8
  58.2 64.0 all-gather.6
  124.8 74.2 all-gather.4
  201.5 74.1 reduce-scatter.1
where the time goes:
time: 309 us; the launch traced here: 308 us
  waiting for transfers between devices  157 us (51%)
  matrix products  57.7 us (19%)
  local copies, waits for them, and re-layouts  33.3 us (11%)
  other arithmetic  19.5 us (6%)
  blocking collectives  18.6 us (6%)
  between operations  13.9 us (4%)
  starting transfers between devices  7.54 us (2%)
    all_gather x1, waiting for transfers between devices, route_experts(): lax.all_gather(incoming.reshape(-1, model_width), 'ctx', axis=0, tiled=True)  61.9 us
    all_gather x1, waiting for transfers between devices, attend_all(): piece_rows = lax.all_gather(stacked, 'exp', axis=1, tiled=True)  44.9 us
    reduce_scatter x1, waiting for transfers between devices, route_experts(): lax.psum_scatter(jnp.dot(hidden_activation, down_local, preferred_element...  31.3 us
    dot_general x1, matrix products, route_experts(): jnp.dot(hidden_activation, down_local, preferred_element_type=jnp.float32)  21.1 us
    all_gather x1, waiting for transfers between devices, attend_all(): everyone = lax.all_gather(paired[None], 'ctx', axis=0, tiled=True)  19.3 us
    all_to_all x1, blocking collectives, route_experts(): lax.all_to_all(outgoing, 'exp', split_axis=0, concat_axis=0, tiled=True)  18.6 us
    dot_general x1, matrix products, attend_all(): jnp.einsum('prhgd,pkhd->phgrk', query_head_rows, key_portion, preferred_e...  13.4 us
    reduce_sum x1, other arithmetic, attend_all(): new_sum = jnp.sum(weights, axis=-1)  11.6 us
  transfers between devices with their start and end apart: 5, of which 4 were waited for; matrix products, arithmetic and copies ran while one was open for 34% of the time, Pallas kernels for 0%

commit v1 on v0

--- a/solution.py
+++ b/solution.py
@@ -2,6 +2,7 @@
 import jax.numpy as jnp
 from jax import lax
 from jax.sharding import PartitionSpec as P
+from jax.lax import all_to_all, axis_size
 
 QUERY_HEADS = 20
 KEY_HEADS = 4
@@ -22,7 +23,14 @@
     listed = block_lists[own_blocks]
     usable = listed != own_blocks
     holder = jnp.minimum(listed, blocks_total - 1 - listed)
-    everyone = lax.all_gather(paired[None], "ctx", axis=0, tiled=True)
+
+    def note_the_digits(v0):
+        num_devices = axis_size("ctx")
+        line_up = tuple((num_devices if src_i == 0 else 1 for src_i in range(v0.ndim)))
+        last = jnp.tile(v0, line_up)
+        return all_to_all(last, "ctx", concat_axis=0, tiled=True, split_axis=0)
+
+    everyone = note_the_digits(paired[None])
     second_half = (listed >= ctx_count).astype(jnp.int32)
     remote = everyone[holder, second_half]
     stacked = jnp.concatenate([paired, remote], axis=0)

time: 309 us -> 375 us (1.21)
  waiting for transfers between devices: 157 us -> 215 us
  starting transfers between devices: 7.54 us -> 16.1 us
    all_to_all x0 -> x1, waiting for transfers between devices: none -> 133 us  [note_the_digits(): return all_to_all(last, 'ctx', concat_axis=0, tiled=True, split_axis=0)]
    all_gather x1, waiting for transfers between devices: 61.9 us -> 5.62 us  [route_experts(): lax.all_gather(incoming.reshape(-1, model_width), 'ctx', axis=0, tiled=True)]
    all_gather x1 -> x0, waiting for transfers between devices: 19.3 us -> none  [attend_all(): everyone = lax.all_gather(paired[None], 'ctx', axis=0, tiled=True)]
    all_to_all x0 -> x1, starting transfers between devices: none -> 8.63 us  [note_the_digits(): return all_to_all(last, 'ctx', concat_axis=0, tiled=True, split_axis=0)]
  transfers between devices with their start and end apart: 5 -> 5, of which waited for: 4 -> 4; matrix products, arithmetic and copies ran while one was open for 34% -> 27% of each run, Pallas kernels for 0% -> 0%
where the time goes in v1:
time: 375 us; the launch traced here: 374 us
  waiting for transfers between devices  215 us (57%)
  matrix products  57.8 us (15%)
  local copies, waits for them, and re-layouts  34.3 us (9%)
  other arithmetic  18.7 us (5%)
  blocking collectives  18.6 us (5%)
  starting transfers between devices  16.1 us (4%)
  between operations  13.9 us (4%)
    all_to_all x1, waiting for transfers between devices, note_the_digits(): return all_to_all(last, 'ctx', concat_axis=0, tiled=True, split_axis=0)  133 us
    all_gather x1, waiting for transfers between devices, attend_all(): piece_rows = lax.all_gather(stacked, 'exp', axis=1, tiled=True)  44.6 us
    reduce_scatter x1, waiting for transfers between devices, route_experts(): lax.psum_scatter(jnp.dot(hidden_activation, down_local, preferred_element...  31.5 us
    dot_general x1, matrix products, route_experts(): jnp.dot(hidden_activation, down_local, preferred_element_type=jnp.float32)  21.2 us
    all_to_all x1, blocking collectives, route_experts(): lax.all_to_all(outgoing, 'exp', split_axis=0, concat_axis=0, tiled=True)  18.6 us
    dot_general x1, matrix products, attend_all(): jnp.einsum('prhgd,pkhd->phgrk', query_head_rows, key_portion, preferred_e...  13.5 us
    reduce_sum x1, other arithmetic, attend_all(): new_sum = jnp.sum(weights, axis=-1)  11.6 us
    dot_general x1, matrix products, attend_all(): jnp.einsum('phgrk,pkhd->phgrd', weights.astype(jnp.bfloat16), value_porti...  10.9 us
  transfers between devices with their start and end apart: 5, of which 4 were waited for; matrix products, arithmetic and copies ran while one was open for 27% of the time, Pallas kernels for 0%

profile of v1, /device:TPU:2, one launch (start us, length us, event | category | flops | bytes accessed | tf_op | source)
XLA Modules:
  0.0 374.4 jit_solution(7002491030464252058)
XLA Ops:
  7.2 0.0 all-gather.5.cloned.1.call-start
  7.2 0.8 fusion.45
  8.0 0.7 iota_compare_fusion.2
  8.7 1.3 fusion.24
  10.0 0.1 copy.28
  10.1 0.1 reduce_window_sum.11
  10.1 0.1 copy.29
  10.2 0.7 select_reduce_fusion
  10.9 1.4 convolution_convert_fusion.1
  12.3 0.5 copy.30
  12.8 18.6 %all_to_all.15 = bf16[16,4,5120]{2,1,0:T(4,128)(2,1)S(1)} all-to-all(bf16[16,4,5120]{2,1,0:T(4,128)(2,1)S(1)} %copy.30), channel_id=1, replica_groups=mesh['ctx'=16,'exp'=16] {'exp'}, dimensions={0} | all-to-all | bytes 1310720 | tf_op jit(solution)/shard_map/all_to_all | solution.py:104
  31.4 1.0 reshape.255
  32.4 0.0 all-gather.5.cloned.1.call-update
  32.4 0.9 constant_dynamic-update-slice_fusion.1
  33.3 0.9 constant_dynamic-update-slice_fusion
  34.3 2.5 tile.2
  36.8 8.6 %all-to-all-start = ((bf16[16,2,64,1024]{3,2,1,0:T(8,128)(2,1)}), bf16[16,2,64,1024]{3,2,1,0:T(8,128)(2,1)}, u32[]{:S(2)}, u32[]{:S(2)}) async-start(bf16[16,2,64,1024]{3,2,1,0:T(8,128)(2,1)} %tile.2), calls=%async_computation | async-start | bytes 8388608 | tf_op jit(solution)/shard_map/all_to_all | solution.py:31
  45.4 0.0 all-gather.3.cloned.1.call-start
  45.4 0.1 fusion.46
  45.5 0.6 gather_fusion
  46.2 133.2 %all-to-all-done = bf16[16,2,64,1024]{3,2,1,0:T(8,128)(2,1)} async-done(((bf16[16,2,64,1024]{3,2,1,0:T(8,128)(2,1)}), bf16[16,2,64,1024]{3,2,1,0:T(8,128)(2,1)}, u32[]{:S(2)}, u32[]{:S(2)}) %all-to-all-start) | async-done | bytes 4194336 | tf_op jit(solution)/shard_map/all_to_all | solution.py:31
  179.4 2.8 gather_fusion.1
  182.2 0.8 pad_maximum_fusion.1
  183.1 0.0 all-gather.3.cloned.1.call-update
  183.1 0.0 reduce-scatter.2.cloned.1.call-start
  183.1 5.6 %all-gather.5.cloned.1.call-done = bf16[1024,5120]{1,0:T(8,128)(2,1)} async-done(((bf16[64,5120]{1,0:T(8,128)(2,1)}), bf16[1024,5120]{1,0:T(8,128)(2,1)}) %all-gather.5.cloned.1.call-update) | async-done | bytes 10485776 | tf_op jit(solution)/shard_map/all_gather | solution.py:105
  188.8 8.6 %fusion.11 = f32[1024,256]{1,0:T(8,128)} fusion(bf16[1024,5120]{1,0:T(8,128)(2,1)} %all-gather.5.cloned.1.call-done, bf16[1,5120,256]{2,1,0:T(8,128)(2,1)} %param.17), kind=kOutput, calls=%fused_computation.20 | convolution fusion | flops 2684354560 | bytes 14155776 | tf_op jit(solution)/shard_map/dot_general | solution.py:106
  197.4 21.2 %convolution_convert_fusion = bf16[1024,5120]{1,0:T(8,128)(2,1)} fusion(bf16[1,256,5120]{2,1,0:T(8,128)(2,1)S(1)} %copy-done, bf16[1024,5120]{1,0:T(8,128)(2,1)} %all-gather.5.cloned.1.call-done, bf16[1,5120,256]{2,1,0:T(8,128)(2,1)} %param.18, f32[1024,256]{1,0:T(8,128)} %fusion.11), kind=kOutput, calls=%fused_computation.9 | convolution fusion | flops 5375524864 | bytes 27262976 | tf_op jit(solution)/shard_map/dot_general | solution.py:110
  218.6 0.0 reduce-scatter.2.cloned.1.call-update
  218.6 1.1 copy-done.3
  219.6 0.8 reshape.253
  220.4 0.1 add_compare_fusion
  220.5 0.1 iota_compare_fusion
  220.6 0.1 broadcast_in_dim.25
  220.8 44.6 %all-gather.3.cloned.1.call-done = bf16[4,1024,1024]{2,1,0:T(8,128)(2,1)} async-done(((bf16[4,64,1024]{2,1,0:T(8,128)(2,1)}), bf16[4,1024,1024]{2,1,0:T(8,128)(2,1)}) %all-gather.3.cloned.1.call-update) | async-done | bytes 8388624 | tf_op jit(solution)/shard_map/all_gather | solution.py:40
  265.4 3.9 %fusion.57 = (bf16[2,1024,1024]{2,1,0:T(8,128)(2,1)S(1)}, bf16[2,1024,1024]{2,1,0:T(8,128)(2,1)S(1)}) fusion(bf16[4,1024,1024]{2,1,0:T(8,128)(2,1)} %all-gather.3.cloned.1.call-done), kind=kLoop, calls=%fused_computation.78 | loop fusion | bytes 16777216 | tf_op jit(solution)/shard_map/slice | solution.py:45
  269.3 3.8 %fusion.7 = (bf16[2,2048,512]{2,1,0:T(8,128)(2,1)}, bf16[2,2048,512]{2,1,0:T(8,128)(2,1)}) fusion(bf16[2,1024,1024]{2,1,0:T(8,128)(2,1)S(1)} %get-tuple-element.4, bf16[2,1024,1024]{2,1,0:T(8,128)(2,1)S(1)} %get-tuple-element.5), kind=kLoop, calls=%fused_computation.15 | loop fusion | flops 16777216 | bytes 16777216 | tf_op jit(solution)/shard_map/concatenate | solution.py:45
  273.0 6.2 %copy.25 = bf16[2,2048,512]{1,2,0:T(8,128)(2,1)} copy(bf16[2,2048,512]{2,1,0:T(8,128)(2,1)} %get-tuple-element.3) | data formatting | bytes 8388608 | tf_op jit(solution)/shard_map/slice | solution.py:49
  279.3 6.3 %copy.22 = bf16[2,2048,512]{1,2,0:T(8,128)(2,1)} copy(bf16[2,2048,512]{2,1,0:T(8,128)(2,1)} %get-tuple-element.2) | data formatting | bytes 8388608 | tf_op jit(solution)/shard_map/slice | solution.py:46
  285.6 13.5 %fusion = (f32[2,4,5,64]{3,2,1,0:T(8,128)S(1)}, f32[2,4,2048,64,5]{2,3,4,1,0:T(8,128)}) fusion(pred[2,64,2048]{2,1,0:T(8,128)(4,1)S(1)} %pad_add_fusion, bf16[2,2048,4,128,1]{1,3,4,2,0:T(8,128)(2,1)} %bitcast.69, bf16[2,64,4,5,128]{4,3,2,1,0:T(8,128)(2,1)S(1)} %reshape.253), kind=kOutput, calls=%fused_computation.4 | convolution fusion | flops 1357903360 | bytes 26093568 | tf_op jit(solution)/shard_map/prhgd,pkhd->phgrk/dot_general | solution.py:53
  299.1 11.6 %fusion.1 = f32[2,4,5,64]{3,2,1,0:T(8,128)} fusion(f32[2,4,2048,64,5]{2,3,4,1,0:T(8,128)} %get-tuple-element.7, f32[2,4,5,64]{3,2,1,0:T(8,128)S(1)} %broadcast_maximum_fusion, pred[2,64,2048]{2,1,0:T(8,128)(4,1)S(1)} %pad_add_fusion), kind=kLoop, calls=%fused_computation.5 | loop fusion | flops 26211840 | bytes 21254144 | tf_op jit(solution)/shard_map/reduce_sum | solution.py:67
  310.7 31.5 %reduce-scatter.2.cloned.1.call-done = bf16[64,5120]{1,0:T(8,128)(2,1)} async-done(((bf16[1024,5120]{1,0:T(8,128)(2,1)}), bf16[64,5120]{1,0:T(8,128)(2,1)}) %reduce-scatter.2.cloned.1.call-update) | async-done | bytes 655376 | tf_op jit(solution)/shard_map/reduce_scatter | solution.py:109
  342.2 2.3 reshape.256
  344.5 7.4 %all-to-all-start.2 = ((bf16[16,4,5120]{2,1,0:T(4,128)(2,1)}), bf16[16,4,5120]{2,1,0:T(4,128)(2,1)S(1)}, u32[]{:S(2)}, u32[]{:S(2)}) async-start(bf16[16,4,5120]{2,1,0:T(4,128)(2,1)} %reshape.256), calls=%async_computation.3 | async-start | bytes 1310720 | tf_op jit(solution)/shard_map/all_to_all | solution.py:117
  351.9 10.9 %divide_convert_fusion = bf16[2,64,4,5,128]{4,1,3,2,0:T(8,128)(2,1)S(1)} fusion(bf16[2,2048,4,128,1]{1,3,4,2,0:T(8,128)(2,1)} %bitcast.70, f32[2,4,2048,64,5]{2,3,4,1,0:T(8,128)} %get-tuple-element.7, f32[2,4,5,64]{3,2,1,0:T(8,128)} %copy-done.4, pred[2,64,2048]{2,1,0:T(8,128)(4,1)S(1)} %pad_add_fusion, f32[2,64,4,5]{1,3,2,0:T(8,128)} %bitcast.71), kind=kOutput, calls=%fused_computation.23 | convolution fusion | flops 1369047040 | bytes 26103808 | tf_op jit(solution)/shard_map/phgrk,pkhd->phgrd/dot_general | solution.py:68
  362.8 1.4 copy.27
  364.2 2.6 convert_element_type.51
  366.8 1.0 fusion.6
  (19 shorter events, 0.1 us)
Async XLA Ops:
  7.2 190.2 %copy-start = (bf16[1,256,5120]{2,1,0:T(8,128)(2,1)S(1)}, bf16[1,256,5120]{2,1,0:T(8,128)(2,1)}, u32[]{:S(2)}) copy-start(bf16[1,256,5120]{2,1,0:T(8,128)(2,1)} %param.19) | copy-start | bytes 7864324
  7.2 181.6 %all-gather.5.cloned.1.call-start = ((), (), s32[]{:S(2)}) async-start(), calls=%async_computation.5 | async-start | bytes 11141120 | tf_op jit(solution)/shard_map/all_gather | solution.py:105
  12.8 32.7 %copy-start.2 = (s32[32]{0:T(128)S(1)}, s32[32]{0:T(128)}, u32[]{:S(2)}) copy-start(s32[32]{0:T(128)} %param.13) | copy-start | bytes 388
  36.8 142.7 %all-to-all-start = ((bf16[16,2,64,1024]{3,2,1,0:T(8,128)(2,1)}), bf16[16,2,64,1024]{3,2,1,0:T(8,128)(2,1)}, u32[]{:S(2)}, u32[]{:S(2)}) async-start(bf16[16,2,64,1024]{3,2,1,0:T(8,128)(2,1)} %tile.2), calls=%async_computation | async-start | bytes 8388608 | tf_op jit(solution)/shard_map/all_to_all | solution.py:31
  45.4 220.0 %all-gather.3.cloned.1.call-start = ((), (), s32[]{:S(2)}) async-start(), calls=%async_computation.4 | async-start | bytes 8912896 | tf_op jit(solution)/shard_map/all_gather | solution.py:40
  183.1 159.1 %reduce-scatter.2.cloned.1.call-start = ((), (), s32[]{:S(2)}) async-start(), calls=%async_computation.6 | async-start | bytes 11141120 | tf_op jit(solution)/shard_map/reduce_scatter | solution.py:109
  218.6 1.1 copy-start.3
  299.1 11.6 %copy-start.4 = (f32[2,4,5,64]{3,2,1,0:T(8,128)}, f32[2,4,5,64]{3,2,1,0:T(8,128)S(1)}, u32[]{:S(2)}) copy-start(f32[2,4,5,64]{3,2,1,0:T(8,128)S(1)} %broadcast_maximum_fusion) | copy-start | bytes 30724
  344.5 22.3 %all-to-all-start.2 = ((bf16[16,4,5120]{2,1,0:T(4,128)(2,1)}), bf16[16,4,5120]{2,1,0:T(4,128)(2,1)S(1)}, u32[]{:S(2)}, u32[]{:S(2)}) async-start(bf16[16,4,5120]{2,1,0:T(4,128)(2,1)} %reshape.256), calls=%async_computation.3 | async-start | bytes 1310720 | tf_op jit(solution)/shard_map/all_to_all | solution.py:117
  351.9 15.9 %copy-start.1 = (bf16[1,256,5120]{2,1,0:T(8,128)(2,1)S(1)}, bf16[1,256,5120]{2,1,0:T(8,128)(2,1)}, u32[]{:S(2)}) copy-start(bf16[1,256,5120]{2,1,0:T(8,128)(2,1)} %param.19) | copy-start | bytes 7864324
Sparse Core Ops, SparseCore 0:
  32.5 156.1 all-gather.4
  191.3 74.0 all-gather.2
  267.9 74.1 reduce-scatter.1
